TPU v7x, 128 devices: a whole 4x4x4 slice. The times are simulated.
128 devices in a mesh: row: 8 (over z, y_lo), col: 16 (over x, y_hi, core).
Axes of the slice: x: 4, y: 4 (y_hi: 2, y_lo: 2; y = y_hi * 2 + y_lo), z: 4, core: 2. Of those that a mesh axis runs over, the one named last changes fastest.
Arguments:
- t2_amps: bfloat16 [16384, 2048], P('row', 'col'), may hold values from -6 to 6
- v_ints: bfloat16 [2048, 32768], P('row', 'col'), may hold values from -0.125 to 0.125
- t2_mask: int32 [128, 16], P('row', 'col'), may hold values 0 or 1
- v_mask: int32 [16, 256], P('row', 'col'), may hold values 0 or 1
Outputs:
- ladder: bfloat16 [16384, 32768], P('row', 'col')
All inputs are finite; a program needn't handle non-finite values. No bound on the sum of `t2_mask` or of `v_mask` on one device may be relied on, other than what follows from the above.
Results may differ from a plain program's by a relative error of at most 0.001.
Values may be sent and summed in bfloat16 or wider, within the bound.
A program may use at most 64 MiB of HBM per device.

v0:
```python
import jax
import jax.numpy as jnp
from jax import lax
from jax.sharding import PartitionSpec as P

TILE = 128


def expand(mask, rows, cols):
    kept = jnp.broadcast_to(mask[:, None, :, None] > 0, (mask.shape[0], TILE, mask.shape[1], TILE))
    return kept.reshape(rows, cols)


def body(t2_amps, v_ints, t2_mask, v_mask):
    masked_t2 = jnp.where(
        expand(t2_mask, t2_amps.shape[0], t2_amps.shape[1]), t2_amps, jnp.zeros_like(t2_amps)
    )
    masked_v = jnp.where(
        expand(v_mask, v_ints.shape[0], v_ints.shape[1]), v_ints, jnp.zeros_like(v_ints)
    )
    amp_whole = lax.all_gather(masked_t2, "col", axis=1, tiled=True)
    result = jnp.dot(
        amp_whole,
        lax.all_gather(masked_v, "row", axis=0, tiled=True),
        preferred_element_type=jnp.float32,
    )
    return result.astype(jnp.bfloat16)


def solution(mesh):
    in_specs = (P("row", "col"), P("row", "col"), P("row", "col"), P("row", "col"))
    out_specs = P("row", "col")
    return jax.shard_map(body, mesh=mesh, in_specs=in_specs, out_specs=out_specs, check_vma=False)
```

profile of v0, /device:TPU:1, one launch (start us, length us, event | category | flops | bytes accessed | tf_op | source)
XLA Modules:
  0.0 295.8 jit_solution(9353750892337013907)
XLA Ops:
  6.5 0.0 all-gather.5.cloned.1.call-start
  6.5 0.7 broadcast_compare_fusion
  7.2 0.2 broadcast_in_dim.26
  7.4 2.5 bitcast_select_fusion
  9.9 0.0 all-gather.5.cloned.1.call-update
  9.9 0.0 all-gather.3.cloned.1.call-start
  10.0 0.7 compare_bitcast_fusion
  10.6 0.1 broadcast_bitcast_fusion
  10.7 2.2 broadcast_select_fusion
  12.9 0.0 all-gather.3.cloned.1.call-update
  12.9 168.7 %all-gather.5.cloned.1.call-done = bf16[2048,2048]{1,0:T(8,128)(2,1)} async-done(((bf16[256,2048]{1,0:T(8,128)(2,1)}), bf16[2048,2048]{1,0:T(8,128)(2,1)}) %all-gather.5.cloned.1.call-update) | async-done | bytes 8388624 | tf_op jit(solution)/shard_map/all_gather | solution.py:24
  181.6 83.9 %all-gather.3.cloned.1.call-done = bf16[2048,2048]{1,0:T(8,128)(2,1)} async-done(((bf16[2048,128]{1,0:T(8,128)(2,1)}), bf16[2048,2048]{1,0:T(8,128)(2,1)}) %all-gather.3.cloned.1.call-update) | async-done | bytes 8388624 | tf_op jit(solution)/shard_map/all_gather | solution.py:21
  265.5 23.5 %convolution_convert_fusion = bf16[2048,2048]{1,0:T(8,128)(2,1)} fusion(bf16[2048,2048]{1,0:T(8,128)(2,1)} %all-gather.3.cloned.1.call-done, bf16[2048,2048]{1,0:T(8,128)(2,1)} %all-gather.5.cloned.1.call-done), kind=kOutput, calls=%fused_computation | convolution fusion | flops 17184063488 | bytes 25165824 | tf_op jit(solution)/shard_map/dot_general | solution.py:22
Async XLA Ops:
  6.5 175.1 %all-gather.5.cloned.1.call-start = ((), (), s32[]{:S(2)}) async-start(), calls=%async_computation.1 | async-start | bytes 9437184 | tf_op jit(solution)/shard_map/all_gather | solution.py:24
  9.9 255.6 %all-gather.3.cloned.1.call-start = ((), (), s32[]{:S(2)}) async-start(), calls=%async_computation | async-start | bytes 8912896 | tf_op jit(solution)/shard_map/all_gather | solution.py:21
Sparse Core Ops, SparseCore 0:
  10.0 171.5 all-gather.4
  183.9 81.5 all-gather.2
where the time goes:
time: 296 us
  waiting for transfers between devices  253 us (85%)
  matrix products  23.5 us (8%)
  between operations  13.4 us (5%)
  other arithmetic  5.99 us (2%)
    all_gather x1, waiting for transfers between devices, body(): lax.all_gather(masked_v, 'row', axis=0, tiled=True)  169 us
    all_gather x1, waiting for transfers between devices, body(): amp_whole = lax.all_gather(masked_t2, 'col', axis=1, tiled=True)  83.9 us
    dot_general x1, matrix products, body(): jnp.dot(amp_whole, lax.all_gather(masked_v, 'row', axis=0, tiled=True), p...  23.5 us
  transfers between devices with their start and end apart: 2, of which 2 were waited for; matrix products, arithmetic and copies ran while one was open for 1% of the time, Pallas kernels for 0%

commit v1 on v0

--- a/solution.py
+++ b/solution.py
@@ -4,6 +4,10 @@
 from jax.sharding import PartitionSpec as P
 
 TILE = 128
+pipes_drive = lambda frame_in, in_dim: jnp.concatenate(
+    lax.all_to_all(jnp.stack([frame_in for _ in range(lax.psum(1, "row"))], axis=0), "row", 0, 0),
+    axis=in_dim,
+)
 
 
 def expand(mask, rows, cols):
@@ -19,11 +23,7 @@
         expand(v_mask, v_ints.shape[0], v_ints.shape[1]), v_ints, jnp.zeros_like(v_ints)
     )
     amp_whole = lax.all_gather(masked_t2, "col", axis=1, tiled=True)
-    result = jnp.dot(
-        amp_whole,
-        lax.all_gather(masked_v, "row", axis=0, tiled=True),
-        preferred_element_type=jnp.float32,
-    )
+    result = jnp.dot(amp_whole, pipes_drive(masked_v, 0), preferred_element_type=jnp.float32)
     return result.astype(jnp.bfloat16)
 
 

time: 296 us -> 173 us (0.58)
  waiting for transfers between devices: 253 us -> 0.02 us
  blocking collectives: 0 us -> 129 us
    all_gather x1 -> x0, waiting for transfers between devices: 169 us -> none  [body(): lax.all_gather(masked_v, 'row', axis=0, tiled=True)]
    all_to_all x0 -> x1, blocking collectives: none -> 129 us  [lax.all_to_all(jnp.stack([frame_in for _ in range(lax.psum(1, 'row'))], a...]
    all_gather x1, waiting for transfers between devices: 83.9 us -> 0.01 us  [body(): amp_whole = lax.all_gather(masked_t2, 'col', axis=1, tiled=True)]
  transfers between devices with their start and end apart: 2 -> 1, of which waited for: 2 -> 0; matrix products, arithmetic and copies ran while one was open for 1% -> 2% of each run, Pallas kernels for 0% -> 0%
where the time goes in v1:
time: 173 us; the launch traced here: 172 us
  blocking collectives  129 us (75%)
  matrix products  23.5 us (14%)
  between operations  13.4 us (8%)
  other arithmetic  5.02 us (3%)
    all_to_all x1, blocking collectives, lax.all_to_all(jnp.stack([frame_in for _ in range(lax.psum(1, 'row'))], a...  129 us
    dot_general x1, matrix products, body(): jnp.dot(amp_whole, pipes_drive(masked_v, 0), preferred_element_type=jnp.f...  23.5 us
  transfers between devices with their start and end apart: 1, of which 0 were waited for; matrix products, arithmetic and copies ran while one was open for 2% of the time, Pallas kernels for 0%

profile of v1, /device:TPU:1, one launch (start us, length us, event | category | flops | bytes accessed | tf_op | source)
XLA Modules:
  0.0 171.9 jit_solution(8047747743320157334)
XLA Ops:
  6.5 0.0 all-gather.2.cloned.1.call-start
  6.5 0.7 compare_bitcast_fusion
  7.2 0.1 broadcast_bitcast_fusion
  7.3 2.2 %broadcast_select_fusion = bf16[2048,128]{1,0:T(8,128)(2,1)} fusion(bf16[2048,128]{1,0:T(8,128)(2,1)} %param.4, pred[2048]{0:T(1024)(128)(4,1)S(1)} %broadcast_bitcast_fusion), kind=kLoop, calls=%fused_computation.2 | loop fusion | flops 262144 | bytes 1050624 | tf_op jit(solution)/shard_map/jit(_where)/select_n | solution.py:19
  9.4 0.0 all-gather.2.cloned.1.call-update
  9.5 0.7 broadcast_compare_fusion
  10.2 0.2 broadcast_in_dim.26
  10.4 1.5 bitcast_select_fusion
  11.9 1.1 stack.2
  12.9 128.6 %all_to_all.5 = bf16[8,256,2048]{2,1,0:T(8,128)(2,1)} all-to-all(bf16[8,256,2048]{2,1,0:T(8,128)(2,1)S(1)} %stack.2), channel_id=1, replica_groups=mesh['row'=8,'col'=16] {'row'}, dimensions={0} | all-to-all | bytes 16777216 | tf_op jit(solution)/shard_map/all_to_all | solution.py:8
  141.6 0.0 all-gather.2.cloned.1.call-done
  141.6 23.5 %convolution_convert_fusion = bf16[2048,2048]{1,0:T(8,128)(2,1)} fusion(bf16[2048,2048]{1,0:T(8,128)(2,1)} %all-gather.2.cloned.1.call-done, bf16[2048,2048]{1,0:T(8,128)(2,1)} %bitcast.11), kind=kOutput, calls=%fused_computation | convolution fusion | flops 17184063488 | bytes 25165824 | tf_op jit(solution)/shard_map/dot_general | solution.py:26
Async XLA Ops:
  6.5 135.0 %all-gather.2.cloned.1.call-start = ((), (), s32[]{:S(2)}) async-start(), calls=%async_computation.1 | async-start | bytes 8912896 | tf_op jit(solution)/shard_map/all_gather | solution.py:25
Sparse Core Ops, SparseCore 0:
  9.6 110.2 all-gather.1
